TPU v7x, 512 devices: a whole 4x8x8 slice. The times are simulated.
512 devices in a mesh: region: 4 (over z_lo), group: 16 (over z_hi, y), loop: 8 (over x, core).
Axes of the slice: x: 4, y: 8, z: 8 (z_hi: 2, z_lo: 4; z = z_hi * 4 + z_lo), core: 2. Of those that a mesh axis runs over, the one named last changes fastest.
Arguments:
- history: float32 [16, 262144], P(None, ('region', 'group', 'loop')), may hold values from -6 to 6
- incident: float32 [4, 262144], P(None, ('region', 'group', 'loop')), may hold values from -6 to 6
- positions: float32 [3, 262144], P(None, ('region', 'group', 'loop')), may hold values from -1 to 1
- area: float32 [262144], P(('region', 'group', 'loop')), may hold values from 0.00390625 to 0.03125
- self_weight: float32 [262144], P(('region', 'group', 'loop')), may hold values from 1 to 2
- pair_target: int32 [512, 24], P(('region', 'group', 'loop')), may hold values from 0 to 31
- pair_source: int32 [512, 24], P(('region', 'group', 'loop')), may hold values from 0 to 7
- pair_lag: int32 [512, 24], P(('region', 'group', 'loop')), may hold values from 1 to 12
- pair_count: int32 [512], P(('region', 'group', 'loop')), may hold values from 16 to 24, as said below
- junc_send: int32 [512, 128], P(('region', 'group', 'loop')), may hold values from 0 to 511
- junc_recv: int32 [512, 128], P(('region', 'group', 'loop')), may hold values from 0 to 511
- junc_gain: float32 [512, 128], P(('region', 'group', 'loop')), may hold values from 0.5 to 2
- adjacency: int32 [512], P(('region', 'group', 'loop')), may hold values from 1 to 3
Outputs:
- density: float32 [4, 262144], P(None, ('region', 'group', 'loop'))
Inputs may be any that keep to these rules, and one draw needn't show every extreme that they name: `pair_count`: each device uses between 16 and 24 of its listed pairs, and some device uses all 24.
All inputs are finite; a program needn't handle non-finite values.
Results may differ from a plain program's by a relative error of at most 0.0003.
Values sent between devices are 32-bit elements; how exact they have to be, the bound alone decides.
No kernel may reach another device: no remote copies, remote signals or barrier semaphores. Data moves between devices by JAX's collectives and lax.ppermute only.
A program may use at most 64 MiB of HBM per device.

v0:
```python
import jax
import jax.numpy as jnp
from jax import lax
from jax.sharding import PartitionSpec as P

HIST = 16
STEPS = 4
soften = 0.25


def spline_mix(frac, rows):
    one_minus = 1.0 - frac
    cube = frac * frac * frac
    square = frac * frac
    first = one_minus * one_minus * one_minus / 6.0
    second = (3.0 * cube - 6.0 * square + 4.0) / 6.0
    third = (-3.0 * cube + 3.0 * square + 3.0 * frac + 1.0) / 6.0
    fourth = cube / 6.0
    return (
        first * rows[3][None, :]
        + second * rows[2][None, :]
        + third * rows[1][None, :]
        + fourth * rows[0][None, :]
    )


def pair_term(target_pos, source_pos, source_area, rows):
    delta = target_pos[:, :, None] - source_pos[:, None, :]
    dist_sq = jnp.sum(delta * delta, axis=0)
    weight = source_area[None, :] * lax.rsqrt(dist_sq + soften)
    frac = dist_sq / (1.0 + dist_sq)
    return jnp.sum(weight * spline_mix(frac, rows), axis=1)


def body(
    history,
    incident,
    positions,
    area,
    self_weight,
    pair_target,
    pair_source,
    pair_lag,
    pair_count,
    junc_send,
    junc_recv,
    junc_gain,
    adjacency,
):
    node_dev = history.shape[1]
    tile_rows = node_dev // 2
    groups = lax.axis_size("group")
    regions = lax.axis_size("region")
    target_pos = lax.all_gather(positions, "group", axis=1, tiled=True)
    source_pos, source_area = (
        lax.all_gather(positions, "loop", axis=1, tiled=True),
        lax.all_gather(area, "loop", axis=0, tiled=True),
    )
    stored = jnp.concatenate([history, jnp.zeros((STEPS, node_dev), jnp.float32)], axis=0)
    partner = (lax.axis_index("region") + adjacency[0]) % regions
    zero = jnp.zeros((), jnp.int32)
    outputs = []
    for step in range(STEPS):
        seen_history = lax.all_gather(stored, "loop", axis=1, tiled=True)

        def pair_fn(index, acc):
            target_row = pair_target[0, index] * tile_rows
            source_row = pair_source[0, index] * node_dev
            start = HIST + step - pair_lag[0, index] - 3
            tile_pos = lax.dynamic_slice(target_pos, (zero, target_row), (3, tile_rows))
            member_pos = lax.dynamic_slice(source_pos, (zero, source_row), (3, node_dev))
            member_area = lax.dynamic_slice(source_area, (source_row,), (node_dev,))
            rows = lax.dynamic_slice(seen_history, (start, source_row), (4, node_dev))
            term = pair_term(tile_pos, member_pos, member_area, rows)
            current = lax.dynamic_slice(acc, (target_row,), (tile_rows,))
            return lax.dynamic_update_slice(acc, current + term, (target_row,))

        partial_value = lax.fori_loop(
            0, pair_count[0], pair_fn, jnp.zeros((groups * node_dev,), jnp.float32)
        )
        field = lax.psum_scatter(partial_value, "group", scatter_dimension=0, tiled=True)
        trace = stored[HIST + step - 1][junc_send[0]]
        traces = lax.all_gather(trace[None, :], "region", axis=0, tiled=True)
        received = lax.dynamic_index_in_dim(traces, partner, 0, keepdims=False)
        junction = jnp.zeros((node_dev,), jnp.float32).at[junc_recv[0]].add(junc_gain[0] * received)
        density_now = (incident[step] - field - junction) / self_weight
        stored = stored.at[HIST + step].set(density_now)
        outputs.append(density_now)
    return jnp.stack(outputs, axis=0)


def solution(mesh):
    in_specs = (
        P(None, ("region", "group", "loop")),
        P(None, ("region", "group", "loop")),
        P(None, ("region", "group", "loop")),
        P(("region", "group", "loop")),
        P(("region", "group", "loop")),
        P(("region", "group", "loop"), None),
        P(("region", "group", "loop"), None),
        P(("region", "group", "loop"), None),
        P(("region", "group", "loop")),
        P(("region", "group", "loop"), None),
        P(("region", "group", "loop"), None),
        P(("region", "group", "loop"), None),
        P(("region", "group", "loop")),
    )
    out_specs = P(None, ("region", "group", "loop"))
    return jax.shard_map(body, mesh=mesh, in_specs=in_specs, out_specs=out_specs, check_vma=False)
```

profile of v0, /device:TPU:64, one launch (start us, length us, event | category | flops | bytes accessed | tf_op | source)
XLA Modules:
  0.0 1410.5 jit_solution(5847321745746539040)
XLA Ops:
  3.4 12.7 all-gather.5
  16.1 1.4 scatter_custom_fusion
  17.6 52.4 %all_gather.34 = f32[3,8192]{1,0:T(4,128)S(1)} all-gather(f32[3,512]{1,0:T(4,128)S(1)} %copy-done.4), channel_id=1, replica_groups=mesh['region'=4,'group'=16,'loop'=8] {'group'}, dimensions={1}, use_global_device_ids=true | all-gather | bytes 104448 | tf_op jit(solution)/shard_map/all_gather | solution.py:54
  70.0 13.1 all_gather.35
  83.1 11.3 all-gather.4
  94.4 13.0 all_gather.36
  107.4 152.6 %while.59 = (s32[]{:T(128)}, f32[8192]{0:T(1024)S(1)}, s32[]{:T(128)}, s32[1,24]{1,0:T(1,128)S(1)}, s32[1,24]{1,0:T(1,128)S(1)}, /*index=5*/f32[4096]{0:T(1024)S...) while((s32[]{:T(128)}, f32[8192]{0:T(1024)S(1)}, ...), condition=%wide.region_3.4_spmd, body=%wide.region_0.3_spmd.sunk | while | flops 4720660 | bytes 1111457 | solution.py:78
  260.0 141.7 %all-reduce.1 = f32[8192]{0:T(1024)S(1)} all-reduce(f32[8192]{0:T(1024)S(1)} %get-tuple-element.853), channel_id=6, replica_groups=mesh['region'=4,'group'=16,'loop'=8] {'group'}, use_global_device_ids=true, to_apply=%region_4.5.clone | all-reduce | flops 8192 | bytes 65536
  403.7 23.8 %all_gather.38 = f32[20,4096]{1,0:T(8,128)S(1)} all-gather(f32[20,512]{1,0:T(8,128)S(1)} %scatter.10), channel_id=1, replica_groups=mesh['region'=4,'group'=16,'loop'=8] {'loop'}, dimensions={1}, use_global_device_ids=true | all-gather | bytes 368640 | tf_op jit(solution)/shard_map/all_gather | solution.py:64
  427.5 152.5 %while.60 = (s32[]{:T(128)}, f32[8192]{0:T(1024)S(1)}, s32[]{:T(128)}, s32[1,24]{1,0:T(1,128)S(1)}, s32[1,24]{1,0:T(1,128)S(1)}, /*index=5*/f32[4096]{0:T(1024)S...) while((s32[]{:T(128)}, f32[8192]{0:T(1024)S(1)}, ...), condition=%wide.region_9.10_spmd, body=%wide.region_6.9_spmd.sunk | while | flops 4720660 | bytes 1111457 | solution.py:78
  580.0 141.7 %all-reduce.2 = f32[8192]{0:T(1024)S(1)} all-reduce(f32[8192]{0:T(1024)S(1)} %get-tuple-element.854), channel_id=7, replica_groups=mesh['region'=4,'group'=16,'loop'=8] {'group'}, use_global_device_ids=true, to_apply=%region_10.11.clone | all-reduce | flops 8192 | bytes 65536
  721.7 1.3 gather_fusion.1
  723.0 24.4 %all-gather.6 = f32[4,1,128]{2,1,0:T(1,128)S(1)} all-gather(f32[1,1,128]{2,1,0:T(1,128)S(1)} %bitcast.187), channel_id=3, replica_groups=mesh['region'=4,'group'=16,'loop'=8] {'region'}, dimensions={0}, use_global_device_ids=true | all-gather | bytes 2560 | tf_op jit(solution)/shard_map/all_gather | solution.py:83
  747.4 1.4 scatter_custom_fusion.1
  748.9 13.0 all_gather.40
  761.9 152.5 %while.61 = (s32[]{:T(128)}, f32[8192]{0:T(1024)S(1)}, s32[]{:T(128)}, s32[1,24]{1,0:T(1,128)S(1)}, s32[1,24]{1,0:T(1,128)S(1)}, /*index=5*/f32[4096]{0:T(1024)S...) while((s32[]{:T(128)}, f32[8192]{0:T(1024)S(1)}, ...), condition=%wide.region_15.16_spmd, body=%wide.region_12.15_spmd.sunk | while | flops 4720660 | bytes 1111457 | solution.py:78
  914.4 141.7 %all-reduce.3 = f32[8192]{0:T(1024)S(1)} all-reduce(f32[8192]{0:T(1024)S(1)} %get-tuple-element.855), channel_id=8, replica_groups=mesh['region'=4,'group'=16,'loop'=8] {'group'}, use_global_device_ids=true, to_apply=%region_16.17.clone | all-reduce | flops 8192 | bytes 65536
  1057.4 19.6 %all-gather.7 = f32[4,1,128]{2,1,0:T(1,128)S(1)} all-gather(f32[1,1,128]{2,1,0:T(1,128)S(1)} %bitcast.188), channel_id=4, replica_groups=mesh['region'=4,'group'=16,'loop'=8] {'region'}, dimensions={0}, use_global_device_ids=true | all-gather | bytes 2560 | tf_op jit(solution)/shard_map/all_gather | solution.py:83
  1076.9 1.4 scatter_custom_fusion.2
  1078.5 13.0 all_gather.42
  1091.5 152.7 %while.62 = (s32[]{:T(128)}, f32[8192]{0:T(1024)S(1)}, s32[]{:T(128)}, s32[1,24]{1,0:T(1,128)S(1)}, s32[1,24]{1,0:T(1,128)S(1)}, /*index=5*/f32[4096]{0:T(1024)S...) while((s32[]{:T(128)}, f32[8192]{0:T(1024)S(1)}, ...), condition=%wide.region_21.22_spmd, body=%wide.region_18.21_spmd.sunk | while | flops 4720660 | bytes 1111457 | solution.py:78
  1244.1 141.7 %all-reduce.4 = f32[8192]{0:T(1024)S(1)} all-reduce(f32[8192]{0:T(1024)S(1)} %get-tuple-element.856), channel_id=9, replica_groups=mesh['region'=4,'group'=16,'loop'=8] {'group'}, use_global_device_ids=true, to_apply=%region_22.23.clone | all-reduce | flops 8192 | bytes 65536
  1387.1 21.3 %all-gather.8 = f32[4,1,128]{2,1,0:T(1,128)S(1)} all-gather(f32[1,1,128]{2,1,0:T(1,128)S(1)} %bitcast.186), channel_id=5, replica_groups=mesh['region'=4,'group'=16,'loop'=8] {'region'}, dimensions={0}, use_global_device_ids=true | all-gather | bytes 2560 | tf_op jit(solution)/shard_map/all_gather | solution.py:83
  1408.4 1.4 scatter_custom_fusion.3
  (658 shorter events, 180.0 us)
Async XLA Ops:
  0.0 94.4 %copy-start.3 = (f32[16,512]{1,0:T(8,128)S(1)}, f32[16,512]{1,0:T(8,128)}, u32[]{:S(2)}) copy-start(f32[16,512]{1,0:T(8,128)} %param.27) | copy-start | bytes 98308
  0.0 16.1 %copy-start.7 = (f32[1,128]{1,0:T(1,128)S(1)}, f32[1,128]{1,0:T(1,128)}, u32[]{:S(2)}) copy-start(f32[1,128]{1,0:T(1,128)} %param.38) | copy-start | bytes 1540
  0.0 16.1 %copy-start.9 = (s32[1,128]{1,0:T(1,128)S(1)}, s32[1,128]{1,0:T(1,128)}, u32[]{:S(2)}) copy-start(s32[1,128]{1,0:T(1,128)} %param.37) | copy-start | bytes 1540
  0.0 17.6 %copy-start.4 = (f32[3,512]{1,0:T(4,128)S(1)}, f32[3,512]{1,0:T(4,128)}, u32[]{:S(2)}) copy-start(f32[3,512]{1,0:T(4,128)} %param.29) | copy-start | bytes 18436
  0.0 83.1 %copy-start.8 = (f32[512]{0:T(512)S(1)}, f32[512]{0:T(512)}, u32[]{:S(2)}) copy-start(f32[512]{0:T(512)} %param.30) | copy-start | bytes 6148
  3.4 103.9 %copy-start = (s32[1,24]{1,0:T(1,128)S(1)}, s32[1,24]{1,0:T(1,128)}, u32[]{:S(2)}) copy-start(s32[1,24]{1,0:T(1,128)} %param.32) | copy-start | bytes 292
  3.4 103.9 %copy-start.1 = (s32[1,24]{1,0:T(1,128)S(1)}, s32[1,24]{1,0:T(1,128)}, u32[]{:S(2)}) copy-start(s32[1,24]{1,0:T(1,128)} %param.33) | copy-start | bytes 292
  3.4 103.9 %copy-start.2 = (s32[1,24]{1,0:T(1,128)S(1)}, s32[1,24]{1,0:T(1,128)}, u32[]{:S(2)}) copy-start(s32[1,24]{1,0:T(1,128)} %param.34) | copy-start | bytes 292
  107.4 296.2 %copy-start.6 = (f32[4,512]{1,0:T(4,128)S(1)}, f32[4,512]{1,0:T(4,128)}, u32[]{:S(2)}) copy-start(f32[4,512]{1,0:T(4,128)} %param.28) | copy-start | bytes 24580
  107.4 296.2 %copy-start.5 = (f32[512]{0:T(512)S(1)}, f32[512]{0:T(512)}, u32[]{:S(2)}) copy-start(f32[512]{0:T(512)} %param.31) | copy-start | bytes 6148
where the time goes:
time: 1420 us; the launch traced here: 1410 us
  blocking collectives  784 us (55%)
  loops' own time  438 us (31%)
  other arithmetic  173 us (12%)
    unnamed x4, blocking collectives  567 us
    another operation x4, loops' own time, body(): lax.fori_loop(0, pair_count[0], pair_fn, jnp.zeros((groups * node_dev,),...  438 us
    all_gather x4, blocking collectives, body(): traces = lax.all_gather(trace[None, :], 'region', axis=0, tiled=True)  77.9 us
    all_gather x4, blocking collectives, body(): seen_history = lax.all_gather(stored, 'loop', axis=1, tiled=True)  62.7 us
    all_gather x1, blocking collectives, body(): target_pos = lax.all_gather(positions, 'group', axis=1, tiled=True)  52.4 us
    sub x68, other arithmetic, pair_fn(): start = HIST + step - pair_lag[0, index] - 3  45.7 us
    mul x68, other arithmetic, pair_fn(): target_row = pair_target[0, index] * tile_rows  45.5 us
    reduce_sum x68, other arithmetic, pair_term(): return jnp.sum(weight * spline_mix(frac, rows), axis=1)  40.8 us

commit v1 on v0

--- a/solution.py
+++ b/solution.py
@@ -80,7 +80,10 @@
         )
         field = lax.psum_scatter(partial_value, "group", scatter_dimension=0, tiled=True)
         trace = stored[HIST + step - 1][junc_send[0]]
-        traces = lax.all_gather(trace[None, :], "region", axis=0, tiled=True)
+        traces = jnp.concatenate(
+            lax.all_to_all(jnp.stack([trace[None, :]] * lax.axis_size("region")), "region", 0, 0),
+            axis=0,
+        )
         received = lax.dynamic_index_in_dim(traces, partner, 0, keepdims=False)
         junction = jnp.zeros((node_dev,), jnp.float32).at[junc_recv[0]].add(junc_gain[0] * received)
         density_now = (incident[step] - field - junction) / self_weight

time: 1420 us -> 1400 us (0.986)
  the two profiles are of different devices: /device:TPU:64 before, /device:TPU:6 now
where the time goes in v1:
time: 1400 us; the launch traced here: 1390 us
  loops' own time  616 us (44%)
  blocking collectives  495 us (35%)
  other arithmetic  234 us (17%)
  starting transfers between devices  22.8 us (2%)
  local copies, waits for them, and re-layouts  19 us (1%)
    another operation x4, loops' own time, body(): lax.fori_loop(0, pair_count[0], pair_fn, jnp.zeros((groups * node_dev,),...  616 us
    unnamed x4, blocking collectives  364 us
    sub x96, other arithmetic, pair_fn(): start = HIST + step - pair_lag[0, index] - 3  60.7 us
    mul x96, other arithmetic, pair_fn(): target_row = pair_target[0, index] * tile_rows  60.7 us
    reduce_sum x96, other arithmetic, pair_term(): return jnp.sum(weight * spline_mix(frac, rows), axis=1)  57.6 us
    all_gather x1, blocking collectives, body(): target_pos = lax.all_gather(positions, 'group', axis=1, tiled=True)  55 us
    all_gather x4, blocking collectives, body(): seen_history = lax.all_gather(stored, 'loop', axis=1, tiled=True)  52.1 us
  transfers between devices with their start and end apart: 4, of which 0 were waited for; matrix products, arithmetic and copies ran while one was open for 4% of the time, Pallas kernels for 0%

profile of v1, /device:TPU:6, one launch (start us, length us, event | category | flops | bytes accessed | tf_op | source)
XLA Modules:
  0.0 1388.5 jit_solution(9254736690736510465)
XLA Ops:
  3.3 7.3 all-to-all-start
  10.6 55.0 %all_gather.22 = f32[3,8192]{1,0:T(4,128)S(1)} all-gather(f32[3,512]{1,0:T(4,128)S(1)} %copy-done.4), channel_id=1, replica_groups=mesh['region'=4,'group'=16,'loop'=8] {'group'}, dimensions={1}, use_global_device_ids=true | all-gather | bytes 104448 | tf_op jit(solution)/shard_map/all_gather | solution.py:54
  65.6 12.8 all_gather.23
  78.4 11.1 all-gather
  89.4 13.0 all_gather.24
  102.5 215.1 %while.59 = (s32[]{:T(128)}, f32[8192]{0:T(1024)S(1)}, s32[]{:T(128)}, s32[1,24]{1,0:T(1,128)S(1)}, s32[1,24]{1,0:T(1,128)S(1)}, /*index=5*/f32[4096]{0:T(1024)S...) while((s32[]{:T(128)}, f32[8192]{0:T(1024)S(1)}, ...), condition=%wide.region_3.4_spmd, body=%wide.region_0.3_spmd.sunk | while | flops 4720660 | bytes 1111457 | solution.py:78
  317.6 91.1 %all-reduce.1 = f32[8192]{0:T(1024)S(1)} all-reduce(f32[8192]{0:T(1024)S(1)} %get-tuple-element.853), channel_id=2, replica_groups=mesh['region'=4,'group'=16,'loop'=8] {'group'}, use_global_device_ids=true, to_apply=%region_4.5.clone | all-reduce | flops 8192 | bytes 65536
  409.3 1.3 dynamic-slice.28
  411.4 1.4 scatter_custom_fusion
  414.2 13.0 all_gather.25
  427.2 216.1 %while.60 = (s32[]{:T(128)}, f32[8192]{0:T(1024)S(1)}, s32[]{:T(128)}, s32[1,24]{1,0:T(1,128)S(1)}, s32[1,24]{1,0:T(1,128)S(1)}, /*index=5*/f32[4096]{0:T(1024)S...) while((s32[]{:T(128)}, f32[8192]{0:T(1024)S(1)}, ...), condition=%wide.region_9.10_spmd, body=%wide.region_6.9_spmd.sunk | while | flops 4720660 | bytes 1111457 | solution.py:78
  643.9 5.1 all-to-all-start.1
  649.0 91.1 %all-reduce.2 = f32[8192]{0:T(1024)S(1)} all-reduce(f32[8192]{0:T(1024)S(1)} %get-tuple-element.854), channel_id=3, replica_groups=mesh['region'=4,'group'=16,'loop'=8] {'group'}, use_global_device_ids=true, to_apply=%region_10.11.clone | all-reduce | flops 8192 | bytes 65536
  740.1 1.4 scatter_custom_fusion.1
  743.0 13.0 all_gather.26
  755.9 214.6 %while.61 = (s32[]{:T(128)}, f32[8192]{0:T(1024)S(1)}, s32[]{:T(128)}, s32[1,24]{1,0:T(1,128)S(1)}, s32[1,24]{1,0:T(1,128)S(1)}, /*index=5*/f32[4096]{0:T(1024)S...) while((s32[]{:T(128)}, f32[8192]{0:T(1024)S(1)}, ...), condition=%wide.region_15.16_spmd, body=%wide.region_12.15_spmd.sunk | while | flops 4720660 | bytes 1111457 | solution.py:78
  971.1 5.3 all-to-all-start.2
  976.4 91.1 %all-reduce.3 = f32[8192]{0:T(1024)S(1)} all-reduce(f32[8192]{0:T(1024)S(1)} %get-tuple-element.855), channel_id=4, replica_groups=mesh['region'=4,'group'=16,'loop'=8] {'group'}, use_global_device_ids=true, to_apply=%region_16.17.clone | all-reduce | flops 8192 | bytes 65536
  1067.5 1.4 scatter_custom_fusion.2
  1070.4 13.2 all_gather.27
  1083.5 206.1 %while.62 = (s32[]{:T(128)}, f32[8192]{0:T(1024)S(1)}, s32[]{:T(128)}, s32[1,24]{1,0:T(1,128)S(1)}, s32[1,24]{1,0:T(1,128)S(1)}, /*index=5*/f32[4096]{0:T(1024)S...) while((s32[]{:T(128)}, f32[8192]{0:T(1024)S(1)}, ...), condition=%wide.region_21.22_spmd, body=%wide.region_18.21_spmd.sunk | while | flops 4720660 | bytes 1111457 | solution.py:78
  1290.2 5.1 all-to-all-start.3
  1295.3 91.1 %all-reduce.4 = f32[8192]{0:T(1024)S(1)} all-reduce(f32[8192]{0:T(1024)S(1)} %get-tuple-element.856), channel_id=5, replica_groups=mesh['region'=4,'group'=16,'loop'=8] {'group'}, use_global_device_ids=true, to_apply=%region_22.23.clone | all-reduce | flops 8192 | bytes 65536
  1386.4 1.4 scatter_custom_fusion.3
  (918 shorter events, 246.2 us)
Async XLA Ops:
  0.0 89.4 %copy-start.3 = (f32[16,512]{1,0:T(8,128)S(1)}, f32[16,512]{1,0:T(8,128)}, u32[]{:S(2)}) copy-start(f32[16,512]{1,0:T(8,128)} %param.27) | copy-start | bytes 98308
  0.0 10.6 copy-start.4
  0.0 78.4 %copy-start.9 = (s32[1,128]{1,0:T(1,128)S(1)}, s32[1,128]{1,0:T(1,128)}, u32[]{:S(2)}) copy-start(s32[1,128]{1,0:T(1,128)} %param.37) | copy-start | bytes 1540
  0.0 78.4 %copy-start.8 = (f32[512]{0:T(512)S(1)}, f32[512]{0:T(512)}, u32[]{:S(2)}) copy-start(f32[512]{0:T(512)} %param.30) | copy-start | bytes 6148
  2.7 99.7 %copy-start = (s32[1,24]{1,0:T(1,128)S(1)}, s32[1,24]{1,0:T(1,128)}, u32[]{:S(2)}) copy-start(s32[1,24]{1,0:T(1,128)} %param.32) | copy-start | bytes 292
  2.7 99.7 %copy-start.1 = (s32[1,24]{1,0:T(1,128)S(1)}, s32[1,24]{1,0:T(1,128)}, u32[]{:S(2)}) copy-start(s32[1,24]{1,0:T(1,128)} %param.33) | copy-start | bytes 292
  2.7 99.7 %copy-start.2 = (s32[1,24]{1,0:T(1,128)S(1)}, s32[1,24]{1,0:T(1,128)}, u32[]{:S(2)}) copy-start(s32[1,24]{1,0:T(1,128)} %param.34) | copy-start | bytes 292
  3.3 408.0 %all-to-all-start = ((f32[4,1,128]{2,1,0:T(1,128)}), f32[4,1,128]{2,1,0:T(1,128)S(1)}, u32[]{:S(2)}, u32[]{:S(2)}) async-start(f32[4,1,128]{2,1,0:T(1,128)} %stack.27), calls=%async_computation | async-start | bytes 4096 | tf_op jit(solution)/shard_map/all_to_all | solution.py:84
  102.4 215.1 %copy-start.6 = (f32[4,512]{1,0:T(4,128)S(1)}, f32[4,512]{1,0:T(4,128)}, u32[]{:S(2)}) copy-start(f32[4,512]{1,0:T(4,128)} %param.28) | copy-start | bytes 24580
  102.4 308.9 %copy-start.7 = (f32[1,128]{1,0:T(1,128)S(1)}, f32[1,128]{1,0:T(1,128)}, u32[]{:S(2)}) copy-start(f32[1,128]{1,0:T(1,128)} %param.38) | copy-start | bytes 1540
  102.5 310.3 %copy-start.5 = (f32[512]{0:T(512)S(1)}, f32[512]{0:T(512)}, u32[]{:S(2)}) copy-start(f32[512]{0:T(512)} %param.31) | copy-start | bytes 6148
  643.9 96.2 %all-to-all-start.1 = ((f32[4,1,128]{2,1,0:T(1,128)}), f32[4,1,128]{2,1,0:T(1,128)S(1)}, u32[]{:S(2)}, u32[]{:S(2)}) async-start(f32[4,1,128]{2,1,0:T(1,128)} %stack.29), calls=%async_computation.1 | async-start | bytes 4096 | tf_op jit(solution)/shard_map/all_to_all | solution.py:84
  971.1 96.4 %all-to-all-start.2 = ((f32[4,1,128]{2,1,0:T(1,128)}), f32[4,1,128]{2,1,0:T(1,128)S(1)}, u32[]{:S(2)}, u32[]{:S(2)}) async-start(f32[4,1,128]{2,1,0:T(1,128)} %stack.31), calls=%async_computation.2 | async-start | bytes 4096 | tf_op jit(solution)/shard_map/all_to_all | solution.py:84
  1290.2 96.2 %all-to-all-start.3 = ((f32[4,1,128]{2,1,0:T(1,128)}), f32[4,1,128]{2,1,0:T(1,128)S(1)}, u32[]{:S(2)}, u32[]{:S(2)}) async-start(f32[4,1,128]{2,1,0:T(1,128)} %stack.33), calls=%async_computation.3 | async-start | bytes 4096 | tf_op jit(solution)/shard_map/all_to_all | solution.py:84
